TPU v7x, 32 devices: a whole 2x2x4 slice. The times are simulated.
32 devices in a mesh: lat: 4 (over z), lon: 8 (over y, x, core).
Axes of the slice: x: 2, y: 2, z: 4, core: 2. Of those that a mesh axis runs over, the one named last changes fastest.
Arguments:
- state_grid: bfloat16 [24, 672, 192], P('lat', 'lon'), may hold values from -6 to 6
- norm_gain: float32 [192], replicated, may hold values from 0.1 to 1.9
- w_qkv: bfloat16 [192, 576], replicated, may hold values from -0.4375 to 0.4375
- w_proj: bfloat16 [192, 192], replicated, may hold values from -1.25 to 1.25
- bias_table: float32 [8, 6, 253], replicated, may hold values from -6 to 300
- window_kind: int32 [4, 56], replicated, may hold values from 0 to 7
- cotangent: bfloat16 [24, 672, 192], P('lat', 'lon'), may hold values from -6 to 6
Outputs:
- out_field: bfloat16 [24, 672, 192], P('lat', 'lon')
- d_field: bfloat16 [24, 672, 192], P('lat', 'lon')
- qkv_grad: float32 [192, 576], replicated
- proj_grad: float32 [192, 192], replicated
- table_grad: float32 [8, 6, 253], replicated
- gain_grad: float32 [192], replicated
All inputs are finite; a program needn't handle non-finite values.
Results may differ from a plain program's by a relative error of at most 0.009.
Values may be sent and summed in bfloat16 or wider, within the bound.
A program may use at most 64 MiB of HBM per device.

v0:
```python
import jax
import jax.numpy as jnp
from jax import lax
from jax.sharding import PartitionSpec as P

HEADS = 6
WIN_LAT = 6
WIN_LON = 12
norm_eps = 1e-05
clip_eps = 1e-06
clip_level = 1.0
masked_score = -1e30
highest = lax.Precision.HIGHEST


def shifted(value, axis, steps):
    count = lax.axis_size(axis)
    pairs = [(source, (source + steps) % count) for source in range(count)]
    return lax.ppermute(value, axis, pairs)


def relation_onehot(win_lat, win_lon):
    position = jnp.arange(win_lat * win_lon, dtype=jnp.int32)
    row_of = position // win_lon
    column = position % win_lon
    offset = (row_of[:, None] - row_of[None, :] + win_lat - 1) * (2 * win_lon - 1) + (
        column[:, None] - column[None, :] + win_lon - 1
    )
    extent = (2 * win_lat - 1) * (2 * win_lon - 1)
    return (offset.reshape(-1)[:, None] == jnp.arange(extent, dtype=jnp.int32)[None, :]).astype(
        jnp.float32
    )


def to_windows(source, win_lat, win_lon):
    rows_all, cols_all, channels = source.shape
    source = source.reshape(rows_all // win_lat, win_lat, cols_all // win_lon, win_lon, channels)
    return source.transpose(0, 2, 1, 3, 4).reshape(-1, win_lat * win_lon, channels)


def from_windows(windows, rows_all, cols_all, win_lat, win_lon):
    channels = windows.shape[-1]
    source = windows.reshape(rows_all // win_lat, cols_all // win_lon, win_lat, win_lon, channels)
    return source.transpose(0, 2, 1, 3, 4).reshape(rows_all, cols_all, channels)


def window_bias(bias_table, kinds_flat, onehot_rel, positions):
    kind_count, heads_n, extent = bias_table.shape
    spread = jnp.einsum(
        "ke,pe->kp",
        bias_table.reshape(kind_count * heads_n, extent),
        onehot_rel,
        precision=highest,
        preferred_element_type=jnp.float32,
    )
    kind_onehot = (kinds_flat[:, None] == jnp.arange(kind_count, dtype=jnp.int32)[None, :]).astype(
        jnp.float32
    )
    per_window = jnp.dot(
        kind_onehot,
        spread.reshape(kind_count, heads_n * positions * positions),
        precision=highest,
        preferred_element_type=jnp.float32,
    )
    return (per_window.reshape(-1, heads_n, positions, positions), kind_onehot)


def attend_forward(x_windows, norm_gain, w_qkv, w_proj, bias_win, allowed):
    count, positions, channels = x_windows.shape
    head_size = channels // HEADS
    inv_sqrt = head_size ** (-0.5)
    flat_rows = x_windows.reshape(-1, channels).astype(jnp.float32)
    centre = flat_rows - jnp.mean(flat_rows, axis=-1, keepdims=True)
    inverse = lax.rsqrt(jnp.mean(centre * centre, axis=-1, keepdims=True) + norm_eps)
    unit_rows = centre * inverse
    normed = (unit_rows * norm_gain).astype(jnp.bfloat16)
    qkv_rows = jnp.dot(normed, w_qkv, preferred_element_type=jnp.float32).astype(jnp.bfloat16)
    parts_qkv = qkv_rows.reshape(count, positions, 3, HEADS, head_size)
    queries = parts_qkv[:, :, 0]
    keys_in = parts_qkv[:, :, 1]
    values_in = parts_qkv[:, :, 2]
    scores = (
        jnp.einsum("wihd,wjhd->whij", queries, keys_in, preferred_element_type=jnp.float32)
        * inv_sqrt
        + bias_win
    )
    scores = jnp.where(allowed, scores, masked_score)
    soft_probs = jax.nn.softmax(scores, axis=-1)
    probs_low = soft_probs.astype(jnp.bfloat16)
    mixed_rows = jnp.einsum(
        "whij,wjhd->wihd", probs_low, values_in, preferred_element_type=jnp.float32
    )
    mixed_rows = mixed_rows.astype(jnp.bfloat16).reshape(-1, channels)
    branch = jnp.dot(mixed_rows, w_proj, preferred_element_type=jnp.float32).astype(jnp.bfloat16)
    saved = (
        normed,
        unit_rows,
        inverse,
        queries,
        keys_in,
        values_in,
        soft_probs,
        probs_low,
        mixed_rows,
    )
    return (saved, branch)


def attend_backward(
    saved, g_windows, keep_win, w_qkv, w_proj, norm_gain, kind_onehot, onehot_rel, table_dims
):
    normed, unit_rows, inverse, queries, keys_in, values_in, soft_probs, probs_low, mixed_rows = (
        saved
    )
    count, heads_n, positions = (soft_probs.shape[0], soft_probs.shape[1], soft_probs.shape[2])
    channels = normed.shape[1]
    head_size = channels // heads_n
    inv_sqrt = head_size ** (-0.5)
    flat_g = g_windows.reshape(-1, channels)
    keep_rows = keep_win.reshape(-1, 1)
    keep_low = keep_rows.astype(jnp.bfloat16)
    grad_proj = jnp.einsum(
        "nc,nd->cd", mixed_rows * keep_low, flat_g, preferred_element_type=jnp.float32
    )
    d_mixed = jnp.einsum("nd,cd->nc", flat_g, w_proj, preferred_element_type=jnp.float32).astype(
        jnp.bfloat16
    )
    d_mixed = d_mixed.reshape(count, positions, heads_n, head_size)
    d_probs = jnp.einsum("wihd,wjhd->whij", d_mixed, values_in, preferred_element_type=jnp.float32)
    d_values = jnp.einsum(
        "whij,wihd->wjhd", probs_low, d_mixed, preferred_element_type=jnp.float32
    ).astype(jnp.bfloat16)
    d_scores = soft_probs * (d_probs - jnp.sum(soft_probs * d_probs, axis=-1, keepdims=True))
    d_scores_low = d_scores.astype(jnp.bfloat16)
    d_queries = (
        jnp.einsum("whij,wjhd->wihd", d_scores_low, keys_in, preferred_element_type=jnp.float32)
        * inv_sqrt
    ).astype(jnp.bfloat16)
    d_keys = (
        jnp.einsum("whij,wihd->wjhd", d_scores_low, queries, preferred_element_type=jnp.float32)
        * inv_sqrt
    ).astype(jnp.bfloat16)
    d_qkv = jnp.stack([d_queries, d_keys, d_values], axis=2).reshape(-1, 3 * channels)
    grad_qkv = jnp.einsum("nc,nd->cd", normed * keep_low, d_qkv, preferred_element_type=jnp.float32)
    d_normed = jnp.einsum("nd,cd->nc", d_qkv, w_qkv, preferred_element_type=jnp.float32)
    grad_gain = jnp.sum(d_normed * unit_rows * keep_rows, axis=0)
    d_unit = d_normed * norm_gain
    d_path = inverse * (
        d_unit
        - jnp.mean(d_unit, axis=-1, keepdims=True)
        - unit_rows * jnp.mean(d_unit * unit_rows, axis=-1, keepdims=True)
    )
    d_path = d_path.astype(jnp.bfloat16)
    query_keep = keep_win.reshape(count, 1, positions, 1)
    by_kind = jnp.einsum(
        "wk,wx->kx",
        kind_onehot,
        (d_scores * query_keep).reshape(count, -1),
        precision=highest,
        preferred_element_type=jnp.float32,
    )
    grad_table = jnp.dot(
        by_kind.reshape(-1, positions * positions),
        onehot_rel,
        precision=highest,
        preferred_element_type=jnp.float32,
    )
    return (d_path, (grad_qkv, grad_proj, grad_table.reshape(table_dims), grad_gain))


def shifted_pair(source, half_lat, half_lon):
    upper = shifted(source[:half_lat], "lat", -1)
    stacked = jnp.concatenate([source[half_lat:], upper], axis=0)
    right_side = shifted(stacked[:, :half_lon], "lon", -1)
    return jnp.concatenate([stacked[:, half_lon:], right_side], axis=1)


def unshift_pair(block, half_lat, half_lon):
    trailing = shifted(block[:, -half_lon:], "lon", 1)
    placed = jnp.concatenate([trailing, block[:, :-half_lon]], axis=1)
    lower = shifted(placed[-half_lat:], "lat", 1)
    return jnp.concatenate([lower, placed[:-half_lat]], axis=0)


def clip_rms(gradient):
    return gradient * jnp.minimum(
        1.0, clip_level * lax.rsqrt(jnp.mean(gradient * gradient) + clip_eps)
    )


def on_device(state_grid, norm_gain, w_qkv, w_proj, bias_table, window_kind, cotangent):
    rows_dev, cols_dev, channels = state_grid.shape
    half_lat = WIN_LAT // 2
    half_lon = WIN_LON // 2
    positions = WIN_LAT * WIN_LON
    lat_index = lax.axis_index("lat")
    lon_index = lax.axis_index("lon")
    rows_all = rows_dev * lax.axis_size("lat")
    onehot_rel = relation_onehot(WIN_LAT, WIN_LON)
    band_start = lat_index * (rows_dev // WIN_LAT)
    sector_start = lon_index * (cols_dev // WIN_LON)
    first_row = lat_index * rows_dev + half_lat
    types_block = lax.dynamic_slice(
        window_kind, (band_start, sector_start), (rows_dev // WIN_LAT, cols_dev // WIN_LON)
    )
    keep_grid = jnp.ones((rows_dev, cols_dev), jnp.float32)
    joint = jnp.concatenate([state_grid, cotangent], axis=2)
    block_joint = shifted_pair(joint, half_lat, half_lon)
    block_x = block_joint[:, :, :channels]
    block_g = block_joint[:, :, channels:]
    block_rows, block_cols = (block_x.shape[0], block_x.shape[1])
    row_ids = (first_row + jnp.arange(block_rows, dtype=jnp.int32)) % rows_all
    labels = (row_ids + half_lat) // WIN_LAT
    label_grid = jnp.broadcast_to(labels[:, None, None], (block_rows, block_cols, 1))
    label_win = to_windows(label_grid, WIN_LAT, WIN_LON)[:, :, 0]
    allowed = (label_win[:, :, None] == label_win[:, None, :])[:, None]
    keep_win = to_windows(keep_grid[:, :, None], WIN_LAT, WIN_LON)[:, :, 0]
    bias_win, kind_onehot = window_bias(bias_table, types_block.reshape(-1), onehot_rel, positions)
    saved, branch = attend_forward(
        to_windows(block_x, WIN_LAT, WIN_LON), norm_gain, w_qkv, w_proj, bias_win, allowed
    )
    branch_grid = from_windows(
        branch.reshape(-1, positions, channels), block_rows, block_cols, WIN_LAT, WIN_LON
    )
    g_windows = to_windows(block_g, WIN_LAT, WIN_LON)
    d_path, grads = attend_backward(
        saved,
        g_windows,
        keep_win,
        w_qkv,
        w_proj,
        norm_gain,
        kind_onehot,
        onehot_rel,
        bias_table.shape,
    )
    path_grid = from_windows(
        d_path.reshape(-1, positions, channels), block_rows, block_cols, WIN_LAT, WIN_LON
    )
    both_own = unshift_pair(jnp.concatenate([branch_grid, path_grid], axis=2), half_lat, half_lon)
    branch_own = both_own[:, :, :channels]
    path_own = both_own[:, :, channels:]
    out_field = (state_grid.astype(jnp.float32) + branch_own.astype(jnp.float32)).astype(
        jnp.bfloat16
    )
    d_field = (cotangent.astype(jnp.float32) + path_own.astype(jnp.float32)).astype(jnp.bfloat16)
    grad_qkv, grad_proj, grad_table, grad_gain = grads
    summed = lax.psum((grad_qkv, grad_proj, grad_table, grad_gain), ("lat", "lon"))
    qkv_grad = clip_rms(summed[0])
    proj_grad = clip_rms(summed[1])
    table_grad = clip_rms(summed[2])
    gain_grad = clip_rms(summed[3])
    return (out_field, d_field, qkv_grad, proj_grad, table_grad, gain_grad)


def solution(mesh):
    in_specs = (P("lat", "lon", None), P(), P(), P(), P(), P(), P("lat", "lon", None))
    out_specs = (P("lat", "lon", None), P("lat", "lon", None), P(), P(), P(), P())
    return jax.shard_map(
        on_device, mesh=mesh, in_specs=in_specs, out_specs=out_specs, check_vma=False
    )
```

profile of v0, /device:TPU:1, one launch (start us, length us, event | category | flops | bytes accessed | tf_op | source)
XLA Modules:
  0.0 259.5 jit_solution(4553154303973583669)
XLA Ops:
  7.2 2.0 fusion.30
  9.2 4.1 %collective-permute-start = (bf16[3,84,384]{2,1,0:T(8,128)(2,1)}, bf16[3,84,384]{2,1,0:T(8,128)(2,1)S(1)}, u32[]{:S(2)}, u32[]{:S(2)}) collective-permute-start(bf16[3,84,384]{2,1,0:T(8,128)(2,1)} %get-tuple-element.17), channel_id=1, source_target_pairs={{0,24},{8,0},{16,8},{24,16},{1,25},{9,1},{17,9},{25,17},{2,26},{10... | collective-permute-start | bytes 580616 | tf_op jit(solution)/shard_map/ppermute | solution.py:19
  14.6 2.6 %convolution_bitcast_fusion = f32[48,5184]{1,0:T(8,128)S(1)} fusion(f32[48,253]{1,0:T(8,128)S(1)} %reshape.225, s32[5184]{0:T(1024)S(1)} %add.155), kind=kOutput, calls=%fused_computation.1 | convolution fusion | flops 756765504 | bytes 1064640 | tf_op jit(solution)/shard_map/ke,pe->kp/dot_general | solution.py:49
  17.9 2.7 %dot_general.63 = f32[6,72,72,8]{2,1,0,3:T(8,128)} reshape(f32[31104,8]{0,1:T(8,128)S(1)} %bitcast.82) | data formatting | bytes 1990656 | tf_op jit(solution)/shard_map/dot_general | solution.py:59
  21.4 2.8 %fusion.6 = f32[7,6,72,72]{3,0,2,1:T(8,128)S(1)} fusion(f32[6,72,72,8]{2,1,0,3:T(8,128)} %dot_general.63, s32[7]{0:T(128)S(1)} %dynamic-slice_bitcast_fusion), kind=kOutput, calls=%fused_computation.7 | convolution fusion | flops 20901944 | bytes 1866268 | tf_op jit(solution)/shard_map/dot_general | solution.py:59
  27.1 2.6 %collective-permute-done.1 = bf16[6,6,384]{2,1,0:T(8,128)(2,1)S(1)} collective-permute-done((bf16[6,6,384]{2,1,0:T(8,128)(2,1)S(1)}, bf16[6,6,384]{2,1,0:T(8,128)(2,1)S(1)}, u32[]{:S(2)}, u32[]{:S(2)}) %collective-permute-start.1) | collective-permute-done | bytes 27680 | tf_op jit(solution)/shard_map/ppermute | solution.py:19
  37.3 2.3 fusion.43
  39.7 2.3 fusion.12
  42.0 1.9 copy.63
  45.2 1.9 convolution_convert_fusion.3
  47.2 1.9 fusion.45
  49.0 1.8 convolution_convert_fusion.4
  50.9 2.0 reshape.230
  52.9 2.3 fusion.13
  55.2 1.8 multiply_reduce_fusion
  63.7 2.2 reshape.233
  68.8 1.9 fusion.2
  72.4 36.5 %all-reduce = (f32[8,6,253]{2,0,1:T(8,128)S(1)}, f32[192]{0:T(256)S(1)}) all-reduce(f32[8,6,253]{2,0,1:T(8,128)S(1)} %fusion.2, f32[192]{0:T(256)S(1)} %get-tuple-element.6), channel_id=1, replica_groups=mesh['lat'=4,'lon'=8] {'lat','lon'}, use_global_device_ids=true, to_apply=%region_11.12 | all-reduce | flops 12336 | bytes 98688 | tf_op jit(solution)/shard_map/psum | solution.py:248
  111.9 3.4 %collective-permute-start.2 = (bf16[6,6,384]{2,1,0:T(8,128)(2,1)S(1)}, bf16[6,6,384]{2,1,0:T(8,128)(2,1)S(1)}, u32[]{:S(2)}, u32[]{:S(2)}) collective-permute-start(bf16[6,6,384]{2,1,0:T(8,128)(2,1)S(1)} %pad_maximum_fusion.5), channel_id=1, source_target_pairs={{0,1},{1,2},{2,3},{3,4},{4,5},{5,6},{6,7},{7,0},{8,9},{9,10},{10,1... | collective-permute-start | bytes 82952 | tf_op jit(solution)/shard_map/ppermute | solution.py:19
  116.8 2.5 collective-permute-start.3
  119.9 4.2 %collective-permute-done.3 = bf16[3,84,384]{2,1,0:T(8,128)(2,1)S(1)} collective-permute-done((bf16[3,84,384]{2,1,0:T(8,128)(2,1)S(1)}, bf16[3,84,384]{2,1,0:T(8,128)(2,1)S(1)}, u32[]{:S(2)}, u32[]{:S(2)}) %collective-permute-start.3) | collective-permute-done | bytes 193568 | tf_op jit(solution)/shard_map/ppermute | solution.py:19
  125.1 120.2 %all-reduce.4.cloned.1.call-done = (f32[192,576]{1,0:T(8,128)}, f32[192,192]{1,0:T(8,128)}) async-done(((f32[192,576]{1,0:T(8,128)}, f32[192,192]{1,0:T(8,128)}), (f32[192,576]{1,0:T(8,128)}, f32[192,192]{1,0:T(8,128)})) %all-reduce.4.cloned.1.call-update) | async-done | bytes 589840 | tf_op jit(solution)/shard_map/psum | solution.py:248
  247.6 1.8 multiply_reduce_fusion.2
  250.1 1.8 broadcast_multiply_fusion
  (121 shorter events, 32.6 us)
Async XLA Ops:
  7.2 26.5 %copy-start = (bf16[192,576]{1,0:T(8,128)(2,1)S(1)}, bf16[192,576]{1,0:T(8,128)(2,1)}, u32[]{:S(2)}) copy-start(bf16[192,576]{1,0:T(8,128)(2,1)} %param.9) | copy-start | bytes 663556
  7.2 238.1 %all-reduce.4.cloned.1.call-start = ((), (), s32[]{:S(2)}) async-start(), calls=%async_computation | async-start | bytes 1376256 | tf_op jit(solution)/shard_map/psum | solution.py:248
  9.2 16.7 %collective-permute-start = (bf16[3,84,384]{2,1,0:T(8,128)(2,1)}, bf16[3,84,384]{2,1,0:T(8,128)(2,1)S(1)}, u32[]{:S(2)}, u32[]{:S(2)}) collective-permute-start(bf16[3,84,384]{2,1,0:T(8,128)(2,1)} %get-tuple-element.17), channel_id=1, source_target_pairs={{0,24},{8,0},{16,8},{24,16},{1,25},{9,1},{17,9},{25,17},{2,26},{10... | collective-permute-start | bytes 580616 | tf_op jit(solution)/shard_map/ppermute | solution.py:19
  13.7 0.9 copy-start.20
  25.9 3.7 %collective-permute-start.1 = (bf16[6,6,384]{2,1,0:T(8,128)(2,1)S(1)}, bf16[6,6,384]{2,1,0:T(8,128)(2,1)S(1)}, u32[]{:S(2)}, u32[]{:S(2)}) collective-permute-start(bf16[6,6,384]{2,1,0:T(8,128)(2,1)S(1)} %pad_maximum_fusion.6), channel_id=1, source_target_pairs={{0,7},{1,0},{2,1},{3,2},{4,3},{5,4},{6,5},{7,6},{8,15},{9,8},{10,9... | collective-permute-start | bytes 82952 | tf_op jit(solution)/shard_map/ppermute | solution.py:19
  35.1 1.6 copy-start.1
  36.0 1.4 copy-start.7
  39.7 2.3 copy-start.18
  52.9 2.3 copy-start.19
  56.9 1.0 copy-start.8
  57.9 1.3 copy-start.6
  60.3 2.3 copy-start.16
  62.8 3.0 %copy-start.10 = (bf16[7,72,1,6,32]{1,4,3,0,2:T(8,128)(2,1)S(1)}, bf16[7,72,1,6,32]{1,4,3,0,2:T(8,128)(2,1)}, u32[]{:S(2)}) copy-start(bf16[7,72,1,6,32]{1,4,3,0,2:T(8,128)(2,1)} %fusion.14) | copy-start | bytes 580612
  62.9 3.0 %copy-start.11 = (bf16[7,72,1,6,32]{1,4,3,0,2:T(8,128)(2,1)S(1)}, bf16[7,72,1,6,32]{1,4,3,0,2:T(8,128)(2,1)}, u32[]{:S(2)}) copy-start(bf16[7,72,1,6,32]{1,4,3,0,2:T(8,128)(2,1)} %fusion.15) | copy-start | bytes 580612
  62.9 3.0 %copy-start.17 = (bf16[7,72,1,6,32]{1,4,3,0,2:T(8,128)(2,1)S(1)}, bf16[7,72,1,6,32]{1,4,3,0,2:T(8,128)(2,1)}, u32[]{:S(2)}) copy-start(bf16[7,72,1,6,32]{1,4,3,0,2:T(8,128)(2,1)} %fusion.13) | copy-start | bytes 580612
  66.1 1.5 copy-start.2
  68.1 2.6 %copy-start.4 = (f32[504,192]{0,1:T(8,128)S(1)}, f32[504,192]{0,1:T(8,128)}, u32[]{:S(2)}) copy-start(f32[504,192]{0,1:T(8,128)} %copy-done.3) | copy-start | bytes 1161220
  68.8 2.4 copy-start.14
  110.8 1.0 copy-start.9
  111.8 12.4 %copy-start.12 = (bf16[6,84,192]{2,1,0:T(8,128)(2,1)S(1)}, bf16[6,84,192]{2,1,0:T(8,128)(2,1)}, u32[]{:S(2)}) copy-start(bf16[6,84,192]{2,1,0:T(8,128)(2,1)} %param.13) | copy-start | bytes 580612
  111.8 12.4 %copy-start.13 = (bf16[6,84,192]{2,1,0:T(8,128)(2,1)S(1)}, bf16[6,84,192]{2,1,0:T(8,128)(2,1)}, u32[]{:S(2)}) copy-start(bf16[6,84,192]{2,1,0:T(8,128)(2,1)} %param.7) | copy-start | bytes 580612
  111.9 4.7 %collective-permute-start.2 = (bf16[6,6,384]{2,1,0:T(8,128)(2,1)S(1)}, bf16[6,6,384]{2,1,0:T(8,128)(2,1)S(1)}, u32[]{:S(2)}, u32[]{:S(2)}) collective-permute-start(bf16[6,6,384]{2,1,0:T(8,128)(2,1)S(1)} %pad_maximum_fusion.5), channel_id=1, source_target_pairs={{0,1},{1,2},{2,3},{3,4},{4,5},{5,6},{6,7},{7,0},{8,9},{9,10},{10,1... | collective-permute-start | bytes 82952 | tf_op jit(solution)/shard_map/ppermute | solution.py:19
  116.8 7.3 %collective-permute-start.3 = (bf16[3,84,384]{2,1,0:T(8,128)(2,1)S(1)}, bf16[3,84,384]{2,1,0:T(8,128)(2,1)S(1)}, u32[]{:S(2)}, u32[]{:S(2)}) collective-permute-start(bf16[3,84,384]{2,1,0:T(8,128)(2,1)S(1)} %get-tuple-element.21), channel_id=1, source_target_pairs={{0,8},{8,16},{16,24},{24,0},{1,9},{9,17},{17,25},{25,1},{2,10},{10... | collective-permute-start | bytes 580616 | tf_op jit(solution)/shard_map/ppermute | solution.py:19
  245.3 6.6 %copy-start.15 = (f32[192,192]{1,0:T(8,128)S(1)}, f32[192,192]{1,0:T(8,128)}, u32[]{:S(2)}) copy-start(f32[192,192]{1,0:T(8,128)} %get-tuple-element.12) | copy-start | bytes 442372
  (4 other events, 3.1 us)
Sparse Core Ops, SparseCore 0:
  116.7 128.5 all-reduce.3
where the time goes:
time: 260 us; the launch traced here: 259 us
  waiting for transfers between devices  127 us (49%)
  blocking collectives  36.5 us (14%)
  local copies, waits for them, and re-layouts  26 us (10%)
  matrix products  25 us (10%)
  between operations  17.3 us (7%)
  other arithmetic  16.6 us (6%)
  starting transfers between devices  11.1 us (4%)
    psum x1, waiting for transfers between devices, on_device(): lax.psum((grad_qkv, grad_proj, grad_table, grad_gain), ('lat', 'lon'))  120 us
    psum x1, blocking collectives, on_device(): lax.psum((grad_qkv, grad_proj, grad_table, grad_gain), ('lat', 'lon'))  36.5 us
    ppermute x4, starting transfers between devices, shifted(): return lax.ppermute(value, axis, pairs)  11.1 us
    ppermute x4, waiting for transfers between devices, shifted(): return lax.ppermute(value, axis, pairs)  6.82 us
  transfers between devices with their start and end apart: 5, of which 3 were waited for; matrix products, arithmetic and copies ran while one was open for 6% of the time, Pallas kernels for 0%

commit v1 on v0

--- a/solution.py
+++ b/solution.py
@@ -245,7 +245,7 @@
     )
     d_field = (cotangent.astype(jnp.float32) + path_own.astype(jnp.float32)).astype(jnp.bfloat16)
     grad_qkv, grad_proj, grad_table, grad_gain = grads
-    summed = lax.psum((grad_qkv, grad_proj, grad_table, grad_gain), ("lat", "lon"))
+    summed = lax.psum(lax.psum((grad_qkv, grad_proj, grad_table, grad_gain), "lon"), "lat")
     qkv_grad = clip_rms(summed[0])
     proj_grad = clip_rms(summed[1])
     table_grad = clip_rms(summed[2])

time: 260 us -> 228 us (0.88)
  waiting for transfers between devices: 127 us -> 94.3 us
    psum x1 -> x2, waiting for transfers between devices: 120 us -> 85.4 us  [the longest x1 49.9 us: on_device(): lax.psum((grad_qkv, grad_proj, grad_table, grad_gain), 'lon')]
    psum x1 -> x2, blocking collectives: 36.5 us -> 35.7 us  [the longest x1 22.6 us: on_device(): lax.psum((grad_qkv, grad_proj, grad_table, grad_gain), 'lon')]
  transfers between devices with their start and end apart: 5 -> 6, of which waited for: 3 -> 5; matrix products, arithmetic and copies ran while one was open for 6% -> 7% of each run, Pallas kernels for 0% -> 0%
where the time goes in v1:
time: 228 us; the launch traced here: 226 us
  waiting for transfers between devices  94.3 us (41%)
  blocking collectives  35.7 us (16%)
  local copies, waits for them, and re-layouts  25.9 us (11%)
  matrix products  25 us (11%)
  between operations  17.4 us (8%)
  other arithmetic  16 us (7%)
  starting transfers between devices  11.8 us (5%)
    psum x1, waiting for transfers between devices, on_device(): lax.psum((grad_qkv, grad_proj, grad_table, grad_gain), 'lon')  49.9 us
    psum x1, waiting for transfers between devices, on_device(): lax.psum(lax.psum((grad_qkv, grad_proj, grad_table, grad_gain), 'lon'), '...  35.5 us
    psum x1, blocking collectives, on_device(): lax.psum((grad_qkv, grad_proj, grad_table, grad_gain), 'lon')  22.6 us
    psum x1, blocking collectives, on_device(): lax.psum(lax.psum((grad_qkv, grad_proj, grad_table, grad_gain), 'lon'), '...  13.2 us
    ppermute x4, starting transfers between devices, shifted(): return lax.ppermute(value, axis, pairs)  11.7 us
    ppermute x4, waiting for transfers between devices, shifted(): return lax.ppermute(value, axis, pairs)  8.91 us
    reduce_sum x4, other arithmetic, clip_rms(): jnp.mean(gradient * gradient) + clip_eps  4.62 us
  transfers between devices with their start and end apart: 6, of which 5 were waited for; matrix products, arithmetic and copies ran while one was open for 7% of the time, Pallas kernels for 0%

profile of v1, /device:TPU:1, one launch (start us, length us, event | category | flops | bytes accessed | tf_op | source)
XLA Modules:
  0.0 226.2 jit_solution(11307566781013489508)
XLA Ops:
  8.5 4.2 %collective-permute-start = (bf16[3,84,384]{2,1,0:T(8,128)(2,1)S(1)}, bf16[3,84,384]{2,1,0:T(8,128)(2,1)S(1)}, u32[]{:S(2)}, u32[]{:S(2)}) collective-permute-start(bf16[3,84,384]{2,1,0:T(8,128)(2,1)S(1)} %get-tuple-element.21), channel_id=1, source_target_pairs={{0,24},{8,0},{16,8},{24,16},{1,25},{9,1},{17,9},{25,17},{2,26},{10... | collective-permute-start | bytes 580616 | tf_op jit(solution)/shard_map/ppermute | solution.py:19
  14.0 2.6 %convolution_bitcast_fusion = f32[48,5184]{1,0:T(8,128)S(1)} fusion(f32[48,253]{1,0:T(8,128)S(1)} %reshape.225, s32[5184]{0:T(1024)S(1)} %add.163), kind=kOutput, calls=%fused_computation.1 | convolution fusion | flops 756765504 | bytes 1064640 | tf_op jit(solution)/shard_map/ke,pe->kp/dot_general | solution.py:49
  17.3 2.7 %dot_general.63 = f32[6,72,72,8]{2,1,0,3:T(8,128)} reshape(f32[31104,8]{0,1:T(8,128)S(1)} %bitcast.82) | data formatting | bytes 1990656 | tf_op jit(solution)/shard_map/dot_general | solution.py:59
  20.8 2.8 %fusion.6 = f32[7,6,72,72]{3,0,2,1:T(8,128)S(1)} fusion(f32[6,72,72,8]{2,1,0,3:T(8,128)} %dot_general.63, s32[7]{0:T(128)S(1)} %dynamic-slice_bitcast_fusion), kind=kOutput, calls=%fused_computation.7 | convolution fusion | flops 20901944 | bytes 1866268 | tf_op jit(solution)/shard_map/dot_general | solution.py:59
  26.5 2.6 %collective-permute-done.1 = bf16[6,6,384]{2,1,0:T(8,128)(2,1)S(1)} collective-permute-done((bf16[6,6,384]{2,1,0:T(8,128)(2,1)S(1)}, bf16[6,6,384]{2,1,0:T(8,128)(2,1)S(1)}, u32[]{:S(2)}, u32[]{:S(2)}) %collective-permute-start.1) | collective-permute-done | bytes 27680 | tf_op jit(solution)/shard_map/ppermute | solution.py:19
  36.8 2.3 %fusion.43 = (f32[7,6,72]{2,1,0:T(8,128)S(1)}, f32[7,6,72,72]{2,3,1,0:T(8,128)S(1)}) fusion(f32[7,6,72,72]{2,3,1,0:T(8,128)S(1)} %add_select_fusion), kind=kOutput, calls=%fused_computation.105 | output fusion | flops 435527 | bytes 1753920 | tf_op jit(solution)/shard_map/sub | solution.py:88
  39.1 2.3 %fusion.12 = bf16[7,72,6,32]{1,3,2,0:T(8,128)(2,1)} fusion(bf16[7,72,1,6,32]{1,0,4,3,2:T(8,128)(2,1)} %get-tuple-element.17, f32[7,6,72]{2,1,0:T(8,128)S(1)} %get-tuple-element.28, f32[7,6,72,72]{2,3,1,0:T(8,128)S(1)} %add_select_fusion), kind=kOutput, calls=%fused_computation.21 | convolution fusion | flops 14687639 | bytes 1270080 | tf_op jit(solution)/shard_map/whij,wjhd->wihd/dot_general | solution.py:90
  41.4 1.9 copy.63
  44.7 1.9 convolution_convert_fusion.3
  46.6 1.9 fusion.45
  48.5 1.8 convolution_convert_fusion.4
  50.3 2.0 reshape.230
  52.3 2.3 %fusion.13 = bf16[7,72,1,6,32]{1,4,3,0,2:T(8,128)(2,1)} fusion(bf16[7,72,6,32]{1,0,3,2:T(8,128)(2,1)} %reshape.230, f32[7,6,72]{2,1,0:T(8,128)} %copy-done.18, f32[7,6,72,72]{2,3,1,0:T(8,128)S(1)} %add_select_fusion), kind=kOutput, calls=%fused_computation.22 | convolution fusion | flops 14687639 | bytes 1270080 | tf_op jit(solution)/shard_map/whij,wihd->wjhd/dot_general | solution.py:130
  54.6 1.7 multiply_reduce_fusion
  63.1 2.2 reshape.233
  68.2 1.9 fusion.2
  71.8 22.6 %all-reduce = (f32[8,6,253]{2,0,1:T(8,128)S(1)}, f32[192]{0:T(256)S(1)}) all-reduce(f32[8,6,253]{2,0,1:T(8,128)S(1)} %fusion.2, f32[192]{0:T(256)S(1)} %get-tuple-element.6), channel_id=1, replica_groups=mesh['lat'=4,'lon'=8] {'lon'}, use_global_device_ids=true, to_apply=%region_13.14 | all-reduce | flops 12336 | bytes 98688 | tf_op jit(solution)/shard_map/psum | solution.py:248
  94.4 13.2 %all-reduce.2 = (f32[8,6,253]{2,0,1:T(8,128)S(1)}, f32[192]{0:T(256)S(1)}) all-reduce(f32[8,6,253]{2,0,1:T(8,128)S(1)} %get-tuple-element.9, f32[192]{0:T(256)S(1)} %get-tuple-element.10), channel_id=1, replica_groups=mesh['lat'=4,'lon'=8] {'lat'}, use_global_device_ids=true, to_apply=%region_14.15 | all-reduce | flops 12336 | bytes 98688 | tf_op jit(solution)/shard_map/psum | solution.py:248
  110.7 5.3 %collective-permute-start.2 = (bf16[6,6,384]{2,1,0:T(8,128)(2,1)S(1)}, bf16[6,6,384]{2,1,0:T(8,128)(2,1)S(1)}, u32[]{:S(2)}, u32[]{:S(2)}) collective-permute-start(bf16[6,6,384]{2,1,0:T(8,128)(2,1)S(1)} %pad_maximum_fusion.5), channel_id=1, source_target_pairs={{0,1},{1,2},{2,3},{3,4},{4,5},{5,6},{6,7},{7,0},{8,9},{9,10},{10,1... | collective-permute-start | bytes 82952 | tf_op jit(solution)/shard_map/ppermute | solution.py:19
  118.5 49.9 %all-reduce.7.cloned.1.call-done = (f32[192,576]{1,0:T(8,128)}, f32[192,192]{1,0:T(8,128)}) async-done(((f32[192,576]{1,0:T(8,128)}, f32[192,192]{1,0:T(8,128)}), (f32[192,576]{1,0:T(8,128)}, f32[192,192]{1,0:T(8,128)})) %all-reduce.7.cloned.1.call-update) | async-done | bytes 589840 | tf_op jit(solution)/shard_map/psum | solution.py:248
  170.3 5.2 %collective-permute-done.3 = bf16[3,84,384]{2,1,0:T(8,128)(2,1)S(1)} collective-permute-done((bf16[3,84,384]{2,1,0:T(8,128)(2,1)S(1)}, bf16[3,84,384]{2,1,0:T(8,128)(2,1)S(1)}, u32[]{:S(2)}, u32[]{:S(2)}) %collective-permute-start.3) | collective-permute-done | bytes 193568 | tf_op jit(solution)/shard_map/ppermute | solution.py:19
  176.5 35.5 %all-reduce.9.cloned.1.call-done = (f32[192,576]{1,0:T(8,128)}, f32[192,192]{1,0:T(8,128)}) async-done(((f32[192,576]{1,0:T(8,128)}, f32[192,192]{1,0:T(8,128)}), (f32[192,576]{1,0:T(8,128)}, f32[192,192]{1,0:T(8,128)})) %all-reduce.9.cloned.1.call-update) | async-done | bytes 589840 | tf_op jit(solution)/shard_map/psum | solution.py:248
  214.3 1.8 multiply_reduce_fusion.2
  216.8 1.8 broadcast_multiply_fusion
  (125 shorter events, 36.3 us)
Async XLA Ops:
  7.2 26.0 %copy-start = (bf16[192,576]{1,0:T(8,128)(2,1)S(1)}, bf16[192,576]{1,0:T(8,128)(2,1)}, u32[]{:S(2)}) copy-start(bf16[192,576]{1,0:T(8,128)(2,1)} %param.9) | copy-start | bytes 663556
  7.2 161.2 %all-reduce.7.cloned.1.call-start = ((), (), s32[]{:S(2)}) async-start(), calls=%async_computation | async-start | bytes 1376256 | tf_op jit(solution)/shard_map/psum | solution.py:248
  8.5 16.8 %collective-permute-start = (bf16[3,84,384]{2,1,0:T(8,128)(2,1)S(1)}, bf16[3,84,384]{2,1,0:T(8,128)(2,1)S(1)}, u32[]{:S(2)}, u32[]{:S(2)}) collective-permute-start(bf16[3,84,384]{2,1,0:T(8,128)(2,1)S(1)} %get-tuple-element.21), channel_id=1, source_target_pairs={{0,24},{8,0},{16,8},{24,16},{1,25},{9,1},{17,9},{25,17},{2,26},{10... | collective-permute-start | bytes 580616 | tf_op jit(solution)/shard_map/ppermute | solution.py:19
  25.4 3.7 %collective-permute-start.1 = (bf16[6,6,384]{2,1,0:T(8,128)(2,1)S(1)}, bf16[6,6,384]{2,1,0:T(8,128)(2,1)S(1)}, u32[]{:S(2)}, u32[]{:S(2)}) collective-permute-start(bf16[6,6,384]{2,1,0:T(8,128)(2,1)S(1)} %pad_maximum_fusion.6), channel_id=1, source_target_pairs={{0,7},{1,0},{2,1},{3,2},{4,3},{5,4},{6,5},{7,6},{8,15},{9,8},{10,9... | collective-permute-start | bytes 82952 | tf_op jit(solution)/shard_map/ppermute | solution.py:19
  34.5 1.6 copy-start.1
  35.4 1.4 copy-start.7
  39.1 2.3 %copy-start.18 = (f32[7,6,72]{2,1,0:T(8,128)}, f32[7,6,72]{2,1,0:T(8,128)S(1)}, u32[]{:S(2)}) copy-start(f32[7,6,72]{2,1,0:T(8,128)S(1)} %get-tuple-element.28) | copy-start | bytes 36292
  52.3 2.3 %copy-start.19 = (f32[7,6,72]{2,1,0:T(8,128)S(1)}, f32[7,6,72]{2,1,0:T(8,128)}, u32[]{:S(2)}) copy-start(f32[7,6,72]{2,1,0:T(8,128)} %copy-done.18) | copy-start | bytes 36292
  56.4 1.0 copy-start.8
  57.4 1.3 copy-start.6
  59.7 2.3 %copy-start.16 = (bf16[504,192]{0,1:T(8,128)(2,1)S(1)}, bf16[504,192]{0,1:T(8,128)(2,1)}, u32[]{:S(2)}) copy-start(bf16[504,192]{0,1:T(8,128)(2,1)} %convolution_convert_fusion.4) | copy-start | bytes 580612
  62.3 3.0 %copy-start.10 = (bf16[7,72,1,6,32]{1,4,3,0,2:T(8,128)(2,1)S(1)}, bf16[7,72,1,6,32]{1,4,3,0,2:T(8,128)(2,1)}, u32[]{:S(2)}) copy-start(bf16[7,72,1,6,32]{1,4,3,0,2:T(8,128)(2,1)} %fusion.14) | copy-start | bytes 580612
  62.3 3.0 %copy-start.11 = (bf16[7,72,1,6,32]{1,4,3,0,2:T(8,128)(2,1)S(1)}, bf16[7,72,1,6,32]{1,4,3,0,2:T(8,128)(2,1)}, u32[]{:S(2)}) copy-start(bf16[7,72,1,6,32]{1,4,3,0,2:T(8,128)(2,1)} %fusion.15) | copy-start | bytes 580612
  62.3 3.0 %copy-start.17 = (bf16[7,72,1,6,32]{1,4,3,0,2:T(8,128)(2,1)S(1)}, bf16[7,72,1,6,32]{1,4,3,0,2:T(8,128)(2,1)}, u32[]{:S(2)}) copy-start(bf16[7,72,1,6,32]{1,4,3,0,2:T(8,128)(2,1)} %fusion.13) | copy-start | bytes 580612
  65.6 1.4 copy-start.2
  67.5 2.6 %copy-start.4 = (f32[504,192]{0,1:T(8,128)S(1)}, f32[504,192]{0,1:T(8,128)}, u32[]{:S(2)}) copy-start(f32[504,192]{0,1:T(8,128)} %copy-done.3) | copy-start | bytes 1161220
  68.2 2.4 %copy-start.14 = (bf16[504,192]{1,0:T(8,128)(2,1)S(1)}, bf16[504,192]{1,0:T(8,128)(2,1)}, u32[]{:S(2)}) copy-start(bf16[504,192]{1,0:T(8,128)(2,1)} %convert_element_type.116) | copy-start | bytes 580612
  109.6 1.0 copy-start.9
  110.0 65.5 %copy-start.12 = (bf16[6,84,192]{2,1,0:T(8,128)(2,1)S(1)}, bf16[6,84,192]{2,1,0:T(8,128)(2,1)}, u32[]{:S(2)}) copy-start(bf16[6,84,192]{2,1,0:T(8,128)(2,1)} %param.13) | copy-start | bytes 580612
  110.1 65.5 %copy-start.13 = (bf16[6,84,192]{2,1,0:T(8,128)(2,1)S(1)}, bf16[6,84,192]{2,1,0:T(8,128)(2,1)}, u32[]{:S(2)}) copy-start(bf16[6,84,192]{2,1,0:T(8,128)(2,1)} %param.7) | copy-start | bytes 580612
  110.1 101.9 %all-reduce.9.cloned.1.call-start = ((), (), s32[]{:S(2)}) async-start(), calls=%async_computation.1 | async-start | bytes 1376256 | tf_op jit(solution)/shard_map/psum | solution.py:248
  110.7 7.6 %collective-permute-start.2 = (bf16[6,6,384]{2,1,0:T(8,128)(2,1)S(1)}, bf16[6,6,384]{2,1,0:T(8,128)(2,1)S(1)}, u32[]{:S(2)}, u32[]{:S(2)}) collective-permute-start(bf16[6,6,384]{2,1,0:T(8,128)(2,1)S(1)} %pad_maximum_fusion.5), channel_id=1, source_target_pairs={{0,1},{1,2},{2,3},{3,4},{4,5},{5,6},{6,7},{7,0},{8,9},{9,10},{10,1... | collective-permute-start | bytes 82952 | tf_op jit(solution)/shard_map/ppermute | solution.py:19
  168.5 7.0 %collective-permute-start.3 = (bf16[3,84,384]{2,1,0:T(8,128)(2,1)S(1)}, bf16[3,84,384]{2,1,0:T(8,128)(2,1)S(1)}, u32[]{:S(2)}, u32[]{:S(2)}) collective-permute-start(bf16[3,84,384]{2,1,0:T(8,128)(2,1)S(1)} %get-tuple-element.25), channel_id=1, source_target_pairs={{0,8},{8,16},{16,24},{24,0},{1,9},{9,17},{17,25},{25,1},{2,10},{10... | collective-permute-start | bytes 580616 | tf_op jit(solution)/shard_map/ppermute | solution.py:19
  212.0 6.6 %copy-start.15 = (f32[192,192]{1,0:T(8,128)S(1)}, f32[192,192]{1,0:T(8,128)}, u32[]{:S(2)}) copy-start(f32[192,192]{1,0:T(8,128)} %get-tuple-element.16) | copy-start | bytes 442372
  (5 other events, 3.9 us)
Sparse Core Ops, SparseCore 0:
  110.2 58.2 all-reduce.6
  170.8 41.0 all-reduce.8
